TPU v7x, 32 devices: a whole 2x2x4 slice. The times are simulated.
32 devices in a mesh: comp: 4 (over y, core), tile: 8 (over z, x).
Axes of the slice: x: 2, y: 2, z: 4, core: 2. Of those that a mesh axis runs over, the one named last changes fastest.
Arguments:
- column_state: float32 [4, 8, 4, 16, 2048], P('comp', 'tile'), may hold values from -6 to 6
- mixing: float32 [2, 4, 16], replicated, may hold values from 0.02 to 0.24
- vertical: float32 [2, 16, 16], replicated, may hold values from -1.5 to 1.5
- flux_coef: float32 [2, 4], replicated, may hold values from 0.5 to 1.5
- atm_block: int32 [4, 8, 16], P('comp', 'tile'), may hold values from 0 to 15
- ocean_block: int32 [4, 8, 16], P('comp', 'tile'), may hold values from 0 to 15
- tile_offset: int32 [4, 8, 16], P('comp', 'tile'), may hold values from 0 to 6
- remap_weights: bfloat16 [4, 8, 16, 128, 128], P('comp', 'tile'), may hold values from 0 to 0.119628906
- ocean_mask: int32 [8, 2048], P('tile'), may hold values 0 or 1
Outputs:
- new_state: float32 [4, 8, 4, 16, 2048], P('comp', 'tile')
Inputs may be any that keep to these rules, and one draw needn't show every extreme that they name: `atm_block`: entries at comp index 3 are not read.
All inputs are finite; a program needn't handle non-finite values. No bound on the sum of `ocean_mask` on one device may be relied on, other than what follows from the above.
Results may differ from a plain program's by a relative error of at most 0.0003.
Values sent between devices are 32-bit elements; how exact they have to be, the bound alone decides.
No kernel may reach another device: no remote copies, remote signals or barrier semaphores. Data moves between devices by JAX's collectives and lax.ppermute only.
A program may use at most 64 MiB of HBM per device.

v0:
```python
import jax
import jax.numpy as jnp
from jax import lax
from jax.sharding import PartitionSpec as P

REACH = 3
SUB = 2


def extended(cells, sides, width):
    for axis, dim in sides:
        count = lax.axis_size(axis)
        head = lax.slice_in_dim(cells, 0, width, axis=dim)
        tail = lax.slice_in_dim(cells, cells.shape[dim] - width, cells.shape[dim], axis=dim)
        cells = jnp.concatenate(
            [
                lax.ppermute(tail, axis, [(i, (i + 1) % count) for i in range(count)]),
                cells,
                lax.ppermute(head, axis, [((i + 1) % count, i) for i in range(count)]),
            ],
            axis=dim,
        )
    return cells


def passed_along(value, axis, steps):
    count = lax.axis_size(axis)
    pairs = [(source, (source + steps) % count) for source in range(count)]
    return lax.ppermute(value, axis, pairs)


def local(
    column_state,
    mixing,
    vertical,
    flux_coef,
    atm_block,
    ocean_block,
    tile_offset,
    remap_weights,
    ocean_mask,
):
    fields = column_state[0, 0]
    cells = fields.shape[2]
    across = remap_weights.shape[3]
    ocean_cells = remap_weights.shape[4]
    oblocks = cells // ocean_cells
    spread = 2 * REACH + 1
    comp_index = lax.axis_index("comp")
    comp_count = lax.axis_size("comp")
    is_atmos = comp_index < comp_count - 1
    group = jnp.where(is_atmos, 0, 1).astype(jnp.int32)
    rates = lax.dynamic_index_in_dim(mixing, group, 0, keepdims=False)[:, :, None]
    operator = lax.dynamic_index_in_dim(vertical, group, 0, keepdims=False)
    for sweep in range(SUB):
        padded = extended(fields, (("tile", 2),), 1)
        fields = fields + rates * (padded[:, :, :-2] + padded[:, :, 2:] - 2.0 * fields)
    mixed = fields + jnp.einsum("lm,kmz->klz", operator, fields, precision=lax.Precision.HIGHEST)
    surface = jnp.tanh(flux_coef[0][:, None] * mixed[:, -1] + flux_coef[1][:, None] * mixed[:, -2])
    rounded = surface.astype(jnp.bfloat16)
    blocks = rounded.reshape(rounded.shape[0], cells // across, across)
    chosen = blocks[:, atm_block[0, 0], :]
    contrib = jnp.einsum(
        "knb,nbj->nkj", chosen, remap_weights[0, 0], preferred_element_type=jnp.float32
    )
    by_offset = (tile_offset[0, 0][:, None] == jnp.arange(spread, dtype=jnp.int32)[None, :]).astype(
        jnp.float32
    )
    by_block = (ocean_block[0, 0][:, None] == jnp.arange(oblocks, dtype=jnp.int32)[None, :]).astype(
        jnp.float32
    )
    buffers = jnp.einsum(
        "nd,no,nkj->dkoj", by_offset, by_block, contrib, precision=lax.Precision.HIGHEST
    )
    buffers = buffers.reshape(spread, rounded.shape[0], cells)
    buffers = jnp.where(is_atmos, buffers, 0.0)
    received = buffers[REACH]
    for offset in range(-REACH, REACH + 1):
        if offset != 0:
            received = received + passed_along(buffers[REACH + offset], "tile", offset)
    received = lax.psum(received, "comp")
    land = ocean_mask[0].astype(jnp.float32)
    atmosphere = mixed.at[:, -1].add(-0.5 * surface)
    ocean = mixed.at[:, 0].add(land[None, :] * received)
    result = jnp.where(is_atmos, atmosphere, ocean)
    return result[None, None]


def solution(mesh):
    placed = (
        P("comp", "tile", None, None, None),
        P(),
        P(),
        P(),
        P("comp", "tile", None),
        P("comp", "tile", None),
        P("comp", "tile", None),
        P("comp", "tile", None, None, None),
        P("tile", None),
    )
    return jax.shard_map(
        local,
        mesh=mesh,
        in_specs=placed,
        out_specs=P("comp", "tile", None, None, None),
        check_vma=False,
    )
```

profile of v0, /device:TPU:0, one launch (start us, length us, event | category | flops | bytes accessed | tf_op | source)
XLA Modules:
  0.0 47.1 jit_solution(6400851959491823201)
XLA Ops:
  0.0 0.0 copy-start
  0.0 1.4 %copy.46 = f32[1,1,4,16,2048]{4,2,3,1,0:T(4,128)S(1)} copy(f32[1,1,4,16,2048]{4,3,2,1,0:T(8,128)} %param.13) | data formatting | bytes 1048576 | tf_op args[0]
  1.4 0.1 fusion.36
  1.5 3.0 %collective-permute-start = (f32[4,16,1]{2,0,1:T(4,128)S(1)}, f32[4,16,1]{2,0,1:T(4,128)S(1)}, u32[]{:S(2)}, u32[]{:S(2)}) collective-permute-start(f32[4,16,1]{2,0,1:T(4,128)S(1)} %get-tuple-element.35), channel_id=1, source_target_pairs={{0,1},{1,2},{2,3},{3,4},{4,5},{5,6},{6,7},{7,0},{8,9},{9,10},{10,1... | collective-permute-start | bytes 776 | tf_op jit(solution)/shard_map/ppermute | solution.py:17
  4.5 3.1 %collective-permute-start.1 = (f32[4,16,1]{2,0,1:T(4,128)S(1)}, f32[4,16,1]{2,0,1:T(4,128)S(1)}, u32[]{:S(2)}, u32[]{:S(2)}) collective-permute-start(f32[4,16,1]{2,0,1:T(4,128)S(1)} %get-tuple-element.36), channel_id=1, source_target_pairs={{1,0},{2,1},{3,2},{4,3},{5,4},{6,5},{7,6},{0,7},{9,8},{10,9},{11,1... | collective-permute-start | bytes 776 | tf_op jit(solution)/shard_map/ppermute | solution.py:19
  7.6 0.0 copy-start.4
  7.6 0.7 %copy-done.4 = f32[2,4]{1,0:T(2,128)S(1)} copy-done((f32[2,4]{1,0:T(2,128)S(1)}, f32[2,4]{1,0:T(2,128)}, u32[]{:S(2)}) %copy-start.4) | copy-done | bytes 56
  8.3 0.0 copy-start.7
  8.3 0.6 %copy-done.7 = s32[1,1,16]{2,1,0:T(1,128)S(1)} copy-done((s32[1,1,16]{2,1,0:T(1,128)S(1)}, s32[1,1,16]{2,1,0:T(1,128)}, u32[]{:S(2)}) %copy-start.7) | copy-done | bytes 88
  9.0 0.0 copy-start.5
  9.0 0.7 %copy-done.5 = s32[1,1,16]{2,1,0:T(1,128)S(1)} copy-done((s32[1,1,16]{2,1,0:T(1,128)S(1)}, s32[1,1,16]{2,1,0:T(1,128)}, u32[]{:S(2)}) %copy-start.5) | copy-done | bytes 88
  9.6 0.7 %copy-done.6 = s32[1,1,16]{2,1,0:T(1,128)S(1)} copy-done((s32[1,1,16]{2,1,0:T(1,128)S(1)}, s32[1,1,16]{2,1,0:T(1,128)}, u32[]{:S(2)}) %copy-start.6) | copy-done | bytes 88
  10.3 0.7 %copy-done.3 = f32[2,4,16]{2,1,0:T(4,128)S(1)} copy-done((f32[2,4,16]{2,1,0:T(4,128)S(1)}, f32[2,4,16]{2,1,0:T(4,128)}, u32[]{:S(2)}) %copy-start.3) | copy-done | bytes 536
  11.0 0.1 copy.13
  11.1 0.0 collective-permute-done
  11.1 0.0 collective-permute-done.1
  11.1 0.6 %fusion.8 = f32[4,16,2048]{2,0,1:T(4,128)S(1)} fusion(f32[4,16,2048]{2,0,1:T(4,128)S(1)} %bitcast.114, f32[4,16,1]{2,0,1:T(4,128)S(1)} %collective-permute-done.1, f32[4,16,1]{2,0,1:T(4,128)S(1)} %collective-permute-done, f32[4,16]{0,1:T(8,128)S(1)} %copy.13), kind=kLoop, calls=%fused_computation.13 | loop fusion | flops 917504 | bytes 1049344 | tf_op jit(solution)/shard_map/add | solution.py:57
  11.7 0.1 fusion.35
  11.8 0.0 collective-permute-start.2
  11.8 4.7 %collective-permute-start.3 = (f32[4,16,1]{2,0,1:T(4,128)S(1)}, f32[4,16,1]{2,0,1:T(4,128)S(1)}, u32[]{:S(2)}, u32[]{:S(2)}) collective-permute-start(f32[4,16,1]{2,0,1:T(4,128)S(1)} %get-tuple-element.34), channel_id=1, source_target_pairs={{1,0},{2,1},{3,2},{4,3},{5,4},{6,5},{7,6},{0,7},{9,8},{10,9},{11,1... | collective-permute-start | bytes 776 | tf_op jit(solution)/shard_map/ppermute | solution.py:19
  16.5 1.9 %collective-permute-done.2 = f32[4,16,1]{2,0,1:T(4,128)S(1)} collective-permute-done((f32[4,16,1]{2,0,1:T(4,128)S(1)}, f32[4,16,1]{2,0,1:T(4,128)S(1)}, u32[]{:S(2)}, u32[]{:S(2)}) %collective-permute-start.2) | collective-permute-done | bytes 288 | tf_op jit(solution)/shard_map/ppermute | solution.py:17
  18.4 0.0 collective-permute-done.3
  18.4 0.6 %fusion.4 = f32[4,16,2048]{2,0,1:T(4,128)S(1)} fusion(f32[4,16,2048]{2,0,1:T(4,128)S(1)} %fusion.8, f32[4,16,1]{2,0,1:T(4,128)S(1)} %collective-permute-done.3, f32[4,16,1]{2,0,1:T(4,128)S(1)} %collective-permute-done.2, f32[4,16]{0,1:T(8,128)S(1)} %copy.13), kind=kLoop, calls=%fused_computation.7 | loop fusion | flops 917504 | bytes 1049344 | tf_op jit(solution)/shard_map/add | solution.py:57
  19.1 0.0 copy-done.2
  19.1 0.9 %fusion.11 = f32[4,2048,16]{1,2,0:T(8,128)S(1)} fusion(f32[4,16,2048]{2,0,1:T(4,128)S(1)} %fusion.4, f32[2,16,16]{2,1,0:T(8,128)S(1)} %copy-done.2, s32[]{:T(128)S(6)} %select_n.39), kind=kOutput, calls=%fused_computation.18 | convolution fusion | flops 25165824 | bytes 1056772 | tf_op jit(solution)/shard_map/lm,kmz->klz/dot_general | solution.py:58
  20.0 0.7 %bitcast_add_fusion = f32[4,16,2048]{2,0,1:T(4,128)S(1)} fusion(f32[4,2048,16]{1,2,0:T(8,128)S(1)} %fusion.11, f32[4,16,2048]{2,0,1:T(4,128)S(1)} %fusion.8, f32[4,16,1]{2,0,1:T(4,128)S(1)} %collective-permute-done.3, f32[4,16,1]{2,0,1:T(4,128)S(1)} %collective-permute-done.2, f32[4,16]{0,1:T(8,128)S(1)} %copy.13), kind=kLoop, calls=%fused_computation.17 | loop fusion | flops 1048576 | bytes 1573632 | tf_op jit(solution)/shard_map/add | solution.py:58
  20.7 0.1 fusion.22
  20.8 0.6 %gather_fusion = bf16[16,4,128]{2,1,0:T(4,128)(2,1)S(1)} fusion(bf16[4,16,128]{2,0,1:T(4,128)(2,1)S(1)} %copy.16, s32[1024]{0:T(1024)S(1)} %pad_clamp_fusion), kind=kCustom, calls=%fused_computation | custom fusion | bytes 32832 | tf_op jit(solution)/shard_map/gather | solution.py:62
  21.4 0.0 copy-done
  21.4 0.2 fusion.9
  21.6 0.3 fusion
  22.0 1.6 %collective-permute-start.4 = (f32[4,2048]{1,0:T(4,128)S(1)}, f32[4,2048]{1,0:T(4,128)S(1)}, u32[]{:S(2)}, u32[]{:S(2)}) collective-permute-start(f32[4,2048]{1,0:T(4,128)S(1)} %bitcast.117), channel_id=1, source_target_pairs={{0,5},{1,6},{2,7},{3,0},{4,1},{5,2},{6,3},{7,4},{8,13},{9,14},{10,... | collective-permute-start | bytes 98312 | tf_op jit(solution)/shard_map/ppermute | solution.py:29
  23.7 1.4 %collective-permute-start.5 = (f32[4,2048]{1,0:T(4,128)S(1)}, f32[4,2048]{1,0:T(4,128)S(1)}, u32[]{:S(2)}, u32[]{:S(2)}) collective-permute-start(f32[4,2048]{1,0:T(4,128)S(1)} %bitcast.115), channel_id=1, source_target_pairs={{0,6},{1,7},{2,0},{3,1},{4,2},{5,3},{6,4},{7,5},{8,14},{9,15},{10,... | collective-permute-start | bytes 98312 | tf_op jit(solution)/shard_map/ppermute | solution.py:29
  25.1 1.9 %collective-permute-start.6 = (f32[4,2048]{1,0:T(4,128)S(1)}, f32[4,2048]{1,0:T(4,128)S(1)}, u32[]{:S(2)}, u32[]{:S(2)}) collective-permute-start(f32[4,2048]{1,0:T(4,128)S(1)} %bitcast.116), channel_id=1, source_target_pairs={{0,7},{1,0},{2,1},{3,2},{4,3},{5,4},{6,5},{7,6},{8,15},{9,8},{10,9... | collective-permute-start | bytes 98312 | tf_op jit(solution)/shard_map/ppermute | solution.py:29
  27.0 0.6 %collective-permute-start.7 = (f32[4,2048]{1,0:T(4,128)S(1)}, f32[4,2048]{1,0:T(4,128)S(1)}, u32[]{:S(2)}, u32[]{:S(2)}) collective-permute-start(f32[4,2048]{1,0:T(4,128)S(1)} %bitcast.118), channel_id=1, source_target_pairs={{0,1},{1,2},{2,3},{3,4},{4,5},{5,6},{6,7},{7,0},{8,9},{9,10},{10,1... | collective-permute-start | bytes 98312 | tf_op jit(solution)/shard_map/ppermute | solution.py:29
  27.6 2.1 %collective-permute-start.8 = (f32[4,2048]{1,0:T(4,128)S(1)}, f32[4,2048]{1,0:T(4,128)S(1)}, u32[]{:S(2)}, u32[]{:S(2)}) collective-permute-start(f32[4,2048]{1,0:T(4,128)S(1)} %bitcast.119), channel_id=1, source_target_pairs={{0,2},{1,3},{2,4},{3,5},{4,6},{5,7},{6,0},{7,1},{8,10},{9,11},{10,... | collective-permute-start | bytes 98312 | tf_op jit(solution)/shard_map/ppermute | solution.py:29
  29.7 0.0 collective-permute-done.4
  29.7 1.5 %collective-permute-start.9 = (f32[4,2048]{1,0:T(4,128)S(1)}, f32[4,2048]{1,0:T(4,128)S(1)}, u32[]{:S(2)}, u32[]{:S(2)}) collective-permute-start(f32[4,2048]{1,0:T(4,128)S(1)} %bitcast.120), channel_id=1, source_target_pairs={{0,3},{1,4},{2,5},{3,6},{4,7},{5,0},{6,1},{7,2},{8,11},{9,12},{10,... | collective-permute-start | bytes 98312 | tf_op jit(solution)/shard_map/ppermute | solution.py:29
  31.2 0.0 copy-done.1
  31.3 0.0 collective-permute-done.5
  31.3 0.0 collective-permute-done.6
  31.3 2.3 %collective-permute-done.7 = f32[4,2048]{1,0:T(4,128)S(1)} collective-permute-done((f32[4,2048]{1,0:T(4,128)S(1)}, f32[4,2048]{1,0:T(4,128)S(1)}, u32[]{:S(2)}, u32[]{:S(2)}) %collective-permute-start.7) | collective-permute-done | bytes 32800 | tf_op jit(solution)/shard_map/ppermute | solution.py:29
  33.6 0.0 collective-permute-done.8
  33.6 1.8 %collective-permute-done.9 = f32[4,2048]{1,0:T(4,128)S(1)} collective-permute-done((f32[4,2048]{1,0:T(4,128)S(1)}, f32[4,2048]{1,0:T(4,128)S(1)}, u32[]{:S(2)}, u32[]{:S(2)}) %collective-permute-start.9) | collective-permute-done | bytes 32800 | tf_op jit(solution)/shard_map/ppermute | solution.py:29
  35.5 10.3 %psum.7 = f32[4,2048]{1,0:T(4,128)S(1)} all-reduce(f32[4,2048]{1,0:T(4,128)S(1)} %fusion.19), channel_id=1, replica_groups=mesh['comp'=4,'tile'=8] {'comp'}, use_global_device_ids=true, to_apply=%region_0.1 | all-reduce | flops 8192 | bytes 65536 | tf_op jit(solution)/shard_map/psum | solution.py:81
  45.8 0.1 add_dynamic-update-slice_fusion
  45.9 0.1 select_bitcast_fusion
  46.0 1.1 %copy.18 = f32[1,1,4,16,2048]{4,3,2,1,0:T(8,128)} copy(f32[1,1,4,16,2048]{4,2,3,1,0:T(4,128)S(1)} %select_bitcast_fusion) | data formatting | bytes 1048576 | tf_op jit(solution)/shard_map/broadcast_in_dim | solution.py:86
  (23 shorter events, 0.3 us)
Async XLA Ops:
  0.0 21.4 %copy-start = (bf16[1,1,16,128,128]{4,3,2,1,0:T(8,128)(2,1)S(1)}, bf16[1,1,16,128,128]{4,3,2,1,0:T(8,128)(2,1)}, u32[]{:S(2)}) copy-start(bf16[1,1,16,128,128]{4,3,2,1,0:T(8,128)(2,1)} %param.20) | copy-start | bytes 1572868
  1.5 9.5 %collective-permute-start = (f32[4,16,1]{2,0,1:T(4,128)S(1)}, f32[4,16,1]{2,0,1:T(4,128)S(1)}, u32[]{:S(2)}, u32[]{:S(2)}) collective-permute-start(f32[4,16,1]{2,0,1:T(4,128)S(1)} %get-tuple-element.35), channel_id=1, source_target_pairs={{0,1},{1,2},{2,3},{3,4},{4,5},{5,6},{6,7},{7,0},{8,9},{9,10},{10,1... | collective-permute-start | bytes 776 | tf_op jit(solution)/shard_map/ppermute | solution.py:17
  4.5 6.5 %collective-permute-start.1 = (f32[4,16,1]{2,0,1:T(4,128)S(1)}, f32[4,16,1]{2,0,1:T(4,128)S(1)}, u32[]{:S(2)}, u32[]{:S(2)}) collective-permute-start(f32[4,16,1]{2,0,1:T(4,128)S(1)} %get-tuple-element.36), channel_id=1, source_target_pairs={{1,0},{2,1},{3,2},{4,3},{5,4},{6,5},{7,6},{0,7},{9,8},{10,9},{11,1... | collective-permute-start | bytes 776 | tf_op jit(solution)/shard_map/ppermute | solution.py:19
  7.6 0.7 %copy-start.4 = (f32[2,4]{1,0:T(2,128)S(1)}, f32[2,4]{1,0:T(2,128)}, u32[]{:S(2)}) copy-start(f32[2,4]{1,0:T(2,128)} %param.16) | copy-start | bytes 100
  8.3 0.7 %copy-start.7 = (s32[1,1,16]{2,1,0:T(1,128)S(1)}, s32[1,1,16]{2,1,0:T(1,128)}, u32[]{:S(2)}) copy-start(s32[1,1,16]{2,1,0:T(1,128)} %param.17) | copy-start | bytes 196
  9.0 0.7 %copy-start.5 = (s32[1,1,16]{2,1,0:T(1,128)S(1)}, s32[1,1,16]{2,1,0:T(1,128)}, u32[]{:S(2)}) copy-start(s32[1,1,16]{2,1,0:T(1,128)} %param.18) | copy-start | bytes 196
  9.6 0.7 %copy-start.6 = (s32[1,1,16]{2,1,0:T(1,128)S(1)}, s32[1,1,16]{2,1,0:T(1,128)}, u32[]{:S(2)}) copy-start(s32[1,1,16]{2,1,0:T(1,128)} %param.19) | copy-start | bytes 196
  10.3 0.7 %copy-start.3 = (f32[2,4,16]{2,1,0:T(4,128)S(1)}, f32[2,4,16]{2,1,0:T(4,128)}, u32[]{:S(2)}) copy-start(f32[2,4,16]{2,1,0:T(4,128)} %param.14) | copy-start | bytes 1540
  11.8 6.6 %collective-permute-start.2 = (f32[4,16,1]{2,0,1:T(4,128)S(1)}, f32[4,16,1]{2,0,1:T(4,128)S(1)}, u32[]{:S(2)}, u32[]{:S(2)}) collective-permute-start(f32[4,16,1]{2,0,1:T(4,128)S(1)} %get-tuple-element.33), channel_id=1, source_target_pairs={{0,1},{1,2},{2,3},{3,4},{4,5},{5,6},{6,7},{7,0},{8,9},{9,10},{10,1... | collective-permute-start | bytes 776 | tf_op jit(solution)/shard_map/ppermute | solution.py:17
  11.8 6.6 %collective-permute-start.3 = (f32[4,16,1]{2,0,1:T(4,128)S(1)}, f32[4,16,1]{2,0,1:T(4,128)S(1)}, u32[]{:S(2)}, u32[]{:S(2)}) collective-permute-start(f32[4,16,1]{2,0,1:T(4,128)S(1)} %get-tuple-element.34), channel_id=1, source_target_pairs={{1,0},{2,1},{3,2},{4,3},{5,4},{6,5},{7,6},{0,7},{9,8},{10,9},{11,1... | collective-permute-start | bytes 776 | tf_op jit(solution)/shard_map/ppermute | solution.py:19
  16.5 2.5 %copy-start.2 = (f32[2,16,16]{2,1,0:T(8,128)S(1)}, f32[2,16,16]{2,1,0:T(8,128)}, u32[]{:S(2)}) copy-start(f32[2,16,16]{2,1,0:T(8,128)} %param.15) | copy-start | bytes 6148
  22.0 7.7 %collective-permute-start.4 = (f32[4,2048]{1,0:T(4,128)S(1)}, f32[4,2048]{1,0:T(4,128)S(1)}, u32[]{:S(2)}, u32[]{:S(2)}) collective-permute-start(f32[4,2048]{1,0:T(4,128)S(1)} %bitcast.117), channel_id=1, source_target_pairs={{0,5},{1,6},{2,7},{3,0},{4,1},{5,2},{6,3},{7,4},{8,13},{9,14},{10,... | collective-permute-start | bytes 98312 | tf_op jit(solution)/shard_map/ppermute | solution.py:29
  23.7 7.6 %collective-permute-start.5 = (f32[4,2048]{1,0:T(4,128)S(1)}, f32[4,2048]{1,0:T(4,128)S(1)}, u32[]{:S(2)}, u32[]{:S(2)}) collective-permute-start(f32[4,2048]{1,0:T(4,128)S(1)} %bitcast.115), channel_id=1, source_target_pairs={{0,6},{1,7},{2,0},{3,1},{4,2},{5,3},{6,4},{7,5},{8,14},{9,15},{10,... | collective-permute-start | bytes 98312 | tf_op jit(solution)/shard_map/ppermute | solution.py:29
  25.1 6.2 %collective-permute-start.6 = (f32[4,2048]{1,0:T(4,128)S(1)}, f32[4,2048]{1,0:T(4,128)S(1)}, u32[]{:S(2)}, u32[]{:S(2)}) collective-permute-start(f32[4,2048]{1,0:T(4,128)S(1)} %bitcast.116), channel_id=1, source_target_pairs={{0,7},{1,0},{2,1},{3,2},{4,3},{5,4},{6,5},{7,6},{8,15},{9,8},{10,9... | collective-permute-start | bytes 98312 | tf_op jit(solution)/shard_map/ppermute | solution.py:29
  27.0 6.7 %collective-permute-start.7 = (f32[4,2048]{1,0:T(4,128)S(1)}, f32[4,2048]{1,0:T(4,128)S(1)}, u32[]{:S(2)}, u32[]{:S(2)}) collective-permute-start(f32[4,2048]{1,0:T(4,128)S(1)} %bitcast.118), channel_id=1, source_target_pairs={{0,1},{1,2},{2,3},{3,4},{4,5},{5,6},{6,7},{7,0},{8,9},{9,10},{10,1... | collective-permute-start | bytes 98312 | tf_op jit(solution)/shard_map/ppermute | solution.py:29
  27.6 6.0 %collective-permute-start.8 = (f32[4,2048]{1,0:T(4,128)S(1)}, f32[4,2048]{1,0:T(4,128)S(1)}, u32[]{:S(2)}, u32[]{:S(2)}) collective-permute-start(f32[4,2048]{1,0:T(4,128)S(1)} %bitcast.119), channel_id=1, source_target_pairs={{0,2},{1,3},{2,4},{3,5},{4,6},{5,7},{6,0},{7,1},{8,10},{9,11},{10,... | collective-permute-start | bytes 98312 | tf_op jit(solution)/shard_map/ppermute | solution.py:29
  29.6 1.5 %copy-start.1 = (s32[1,2048]{1,0:T(1,128)S(1)}, s32[1,2048]{1,0:T(1,128)}, u32[]{:S(2)}) copy-start(s32[1,2048]{1,0:T(1,128)} %param.21) | copy-start | bytes 24580
  29.7 5.8 %collective-permute-start.9 = (f32[4,2048]{1,0:T(4,128)S(1)}, f32[4,2048]{1,0:T(4,128)S(1)}, u32[]{:S(2)}, u32[]{:S(2)}) collective-permute-start(f32[4,2048]{1,0:T(4,128)S(1)} %bitcast.120), channel_id=1, source_target_pairs={{0,3},{1,4},{2,5},{3,6},{4,7},{5,0},{6,1},{7,2},{8,11},{9,12},{10,... | collective-permute-start | bytes 98312 | tf_op jit(solution)/shard_map/ppermute | solution.py:29
where the time goes:
time: 47.4 us; the launch traced here: 47.1 us
  starting transfers between devices  19.9 us (42%)
  blocking collectives  10.3 us (22%)
  local copies, waits for them, and re-layouts  6.88 us (15%)
  waiting for transfers between devices  6.07 us (13%)
  other arithmetic  2.36 us (5%)
  matrix products  1.45 us (3%)
    psum x1, blocking collectives, local(): received = lax.psum(received, 'comp')  10.3 us
    ppermute x6, starting transfers between devices, passed_along(): return lax.ppermute(value, axis, pairs)  9.11 us
    ppermute x2, starting transfers between devices, extended(): lax.ppermute(head, axis, [((i + 1) % count, i) for i in range(count)])  7.81 us
    unnamed x26, local copies, waits for them, and re-layouts  4.92 us
    ppermute x6, waiting for transfers between devices, passed_along(): return lax.ppermute(value, axis, pairs)  4.18 us
    ppermute x2, starting transfers between devices, extended(): lax.ppermute(tail, axis, [(i, (i + 1) % count) for i in range(count)])  3.02 us
    ppermute x2, waiting for transfers between devices, extended(): lax.ppermute(tail, axis, [(i, (i + 1) % count) for i in range(count)])  1.88 us
    add x2, other arithmetic, local(): fields + rates * (padded[:, :, :-2] + padded[:, :, 2:] - 2.0 * fields)  1.28 us
  transfers between devices with their start and end apart: 10, of which 3 were waited for; matrix products, arithmetic and copies ran while one was open for 0% of the time, Pallas kernels for 0%

commit v1 on v0

--- a/solution.py
+++ b/solution.py
@@ -78,7 +78,12 @@
     for offset in range(-REACH, REACH + 1):
         if offset != 0:
             received = received + passed_along(buffers[REACH + offset], "tile", offset)
-    received = lax.psum(received, "comp")
+    size = lax.axis_size("comp")
+    total, far = (received, 1)
+    while far < size:
+        total = total + lax.ppermute(total, "comp", [(i_2, i_2 ^ far) for i_2 in range(size)])
+        far = 2 * far
+    received = total
     land = ocean_mask[0].astype(jnp.float32)
     atmosphere = mixed.at[:, -1].add(-0.5 * surface)
     ocean = mixed.at[:, 0].add(land[None, :] * received)

time: 47.4 us -> 42.4 us (0.89)
  blocking collectives: 10.3 us -> 0 us
  waiting for transfers between devices: 6.07 us -> 9.55 us
  starting transfers between devices: 19.9 us -> 21.7 us
    psum x1 -> x0, blocking collectives: 10.3 us -> none  [local(): received = lax.psum(received, 'comp')]
    ppermute x0 -> x2, waiting for transfers between devices: none -> 3.4 us  [local(): lax.ppermute(total, 'comp', [(i_2, i_2 ^ far) for i_2 in range(size)])]
    ppermute x0 -> x2, starting transfers between devices: none -> 1.78 us  [local(): lax.ppermute(total, 'comp', [(i_2, i_2 ^ far) for i_2 in range(size)])]
  transfers between devices with their start and end apart: 10 -> 12, of which waited for: 3 -> 5; matrix products, arithmetic and copies ran while one was open for 0% -> 1% of each run, Pallas kernels for 0% -> 0%
where the time goes in v1:
time: 42.4 us; the launch traced here: 42.1 us
  starting transfers between devices  21.7 us (51%)
  waiting for transfers between devices  9.55 us (23%)
  local copies, waits for them, and re-layouts  6.88 us (16%)
  other arithmetic  2.37 us (6%)
  matrix products  1.45 us (3%)
    ppermute x6, starting transfers between devices, passed_along(): return lax.ppermute(value, axis, pairs)  9.11 us
    ppermute x2, starting transfers between devices, extended(): lax.ppermute(head, axis, [((i + 1) % count, i) for i in range(count)])  7.81 us
    unnamed x26, local copies, waits for them, and re-layouts  4.92 us
    ppermute x6, waiting for transfers between devices, passed_along(): return lax.ppermute(value, axis, pairs)  4.26 us
    ppermute x2, waiting for transfers between devices, local(): lax.ppermute(total, 'comp', [(i_2, i_2 ^ far) for i_2 in range(size)])  3.4 us
    ppermute x2, starting transfers between devices, extended(): lax.ppermute(tail, axis, [(i, (i + 1) % count) for i in range(count)])  3.02 us
    ppermute x2, waiting for transfers between devices, extended(): lax.ppermute(tail, axis, [(i, (i + 1) % count) for i in range(count)])  1.88 us
    ppermute x2, starting transfers between devices, local(): lax.ppermute(total, 'comp', [(i_2, i_2 ^ far) for i_2 in range(size)])  1.78 us
  transfers between devices with their start and end apart: 12, of which 5 were waited for; matrix products, arithmetic and copies ran while one was open for 1% of the time, Pallas kernels for 0%

profile of v1, /device:TPU:0, one launch (start us, length us, event | category | flops | bytes accessed | tf_op | source)
XLA Modules:
  0.0 42.1 jit_solution(11763132214596937610)
XLA Ops:
  0.0 0.0 copy-start
  0.0 1.4 %copy.46 = f32[1,1,4,16,2048]{4,2,3,1,0:T(4,128)S(1)} copy(f32[1,1,4,16,2048]{4,3,2,1,0:T(8,128)} %param.13) | data formatting | bytes 1048576 | tf_op args[0]
  1.4 0.1 fusion.36
  1.5 3.0 %collective-permute-start = (f32[4,16,1]{2,0,1:T(4,128)S(1)}, f32[4,16,1]{2,0,1:T(4,128)S(1)}, u32[]{:S(2)}, u32[]{:S(2)}) collective-permute-start(f32[4,16,1]{2,0,1:T(4,128)S(1)} %get-tuple-element.35), channel_id=1, source_target_pairs={{0,1},{1,2},{2,3},{3,4},{4,5},{5,6},{6,7},{7,0},{8,9},{9,10},{10,1... | collective-permute-start | bytes 776 | tf_op jit(solution)/shard_map/ppermute | solution.py:17
  4.5 3.1 %collective-permute-start.1 = (f32[4,16,1]{2,0,1:T(4,128)S(1)}, f32[4,16,1]{2,0,1:T(4,128)S(1)}, u32[]{:S(2)}, u32[]{:S(2)}) collective-permute-start(f32[4,16,1]{2,0,1:T(4,128)S(1)} %get-tuple-element.36), channel_id=1, source_target_pairs={{1,0},{2,1},{3,2},{4,3},{5,4},{6,5},{7,6},{0,7},{9,8},{10,9},{11,1... | collective-permute-start | bytes 776 | tf_op jit(solution)/shard_map/ppermute | solution.py:19
  7.6 0.7 %copy-done.4 = f32[2,4]{1,0:T(2,128)S(1)} copy-done((f32[2,4]{1,0:T(2,128)S(1)}, f32[2,4]{1,0:T(2,128)}, u32[]{:S(2)}) %copy-start.4) | copy-done | bytes 56
  8.3 0.6 %copy-done.7 = s32[1,1,16]{2,1,0:T(1,128)S(1)} copy-done((s32[1,1,16]{2,1,0:T(1,128)S(1)}, s32[1,1,16]{2,1,0:T(1,128)}, u32[]{:S(2)}) %copy-start.7) | copy-done | bytes 88
  9.0 0.7 %copy-done.5 = s32[1,1,16]{2,1,0:T(1,128)S(1)} copy-done((s32[1,1,16]{2,1,0:T(1,128)S(1)}, s32[1,1,16]{2,1,0:T(1,128)}, u32[]{:S(2)}) %copy-start.5) | copy-done | bytes 88
  9.6 0.7 %copy-done.6 = s32[1,1,16]{2,1,0:T(1,128)S(1)} copy-done((s32[1,1,16]{2,1,0:T(1,128)S(1)}, s32[1,1,16]{2,1,0:T(1,128)}, u32[]{:S(2)}) %copy-start.6) | copy-done | bytes 88
  10.3 0.7 %copy-done.3 = f32[2,4,16]{2,1,0:T(4,128)S(1)} copy-done((f32[2,4,16]{2,1,0:T(4,128)S(1)}, f32[2,4,16]{2,1,0:T(4,128)}, u32[]{:S(2)}) %copy-start.3) | copy-done | bytes 536
  11.0 0.1 copy.13
  11.1 0.0 collective-permute-done
  11.1 0.0 collective-permute-done.1
  11.1 0.6 %fusion.8 = f32[4,16,2048]{2,0,1:T(4,128)S(1)} fusion(f32[4,16,2048]{2,0,1:T(4,128)S(1)} %bitcast.114, f32[4,16,1]{2,0,1:T(4,128)S(1)} %collective-permute-done.1, f32[4,16,1]{2,0,1:T(4,128)S(1)} %collective-permute-done, f32[4,16]{0,1:T(8,128)S(1)} %copy.13), kind=kLoop, calls=%fused_computation.13 | loop fusion | flops 917504 | bytes 1049344 | tf_op jit(solution)/shard_map/add | solution.py:57
  11.7 0.1 fusion.35
  11.8 0.0 collective-permute-start.2
  11.8 4.7 %collective-permute-start.3 = (f32[4,16,1]{2,0,1:T(4,128)S(1)}, f32[4,16,1]{2,0,1:T(4,128)S(1)}, u32[]{:S(2)}, u32[]{:S(2)}) collective-permute-start(f32[4,16,1]{2,0,1:T(4,128)S(1)} %get-tuple-element.34), channel_id=1, source_target_pairs={{1,0},{2,1},{3,2},{4,3},{5,4},{6,5},{7,6},{0,7},{9,8},{10,9},{11,1... | collective-permute-start | bytes 776 | tf_op jit(solution)/shard_map/ppermute | solution.py:19
  16.5 1.9 %collective-permute-done.2 = f32[4,16,1]{2,0,1:T(4,128)S(1)} collective-permute-done((f32[4,16,1]{2,0,1:T(4,128)S(1)}, f32[4,16,1]{2,0,1:T(4,128)S(1)}, u32[]{:S(2)}, u32[]{:S(2)}) %collective-permute-start.2) | collective-permute-done | bytes 288 | tf_op jit(solution)/shard_map/ppermute | solution.py:17
  18.4 0.0 collective-permute-done.3
  18.4 0.6 %fusion.4 = f32[4,16,2048]{2,0,1:T(4,128)S(1)} fusion(f32[4,16,2048]{2,0,1:T(4,128)S(1)} %fusion.8, f32[4,16,1]{2,0,1:T(4,128)S(1)} %collective-permute-done.3, f32[4,16,1]{2,0,1:T(4,128)S(1)} %collective-permute-done.2, f32[4,16]{0,1:T(8,128)S(1)} %copy.13), kind=kLoop, calls=%fused_computation.7 | loop fusion | flops 917504 | bytes 1049344 | tf_op jit(solution)/shard_map/add | solution.py:57
  19.1 0.0 copy-done.2
  19.1 0.9 %fusion.11 = f32[4,2048,16]{1,2,0:T(8,128)S(1)} fusion(f32[4,16,2048]{2,0,1:T(4,128)S(1)} %fusion.4, f32[2,16,16]{2,1,0:T(8,128)S(1)} %copy-done.2, s32[]{:T(128)S(6)} %select_n.39), kind=kOutput, calls=%fused_computation.18 | convolution fusion | flops 25165824 | bytes 1056772 | tf_op jit(solution)/shard_map/lm,kmz->klz/dot_general | solution.py:58
  20.0 0.7 %bitcast_add_fusion = f32[4,16,2048]{2,0,1:T(4,128)S(1)} fusion(f32[4,2048,16]{1,2,0:T(8,128)S(1)} %fusion.11, f32[4,16,2048]{2,0,1:T(4,128)S(1)} %fusion.8, f32[4,16,1]{2,0,1:T(4,128)S(1)} %collective-permute-done.3, f32[4,16,1]{2,0,1:T(4,128)S(1)} %collective-permute-done.2, f32[4,16]{0,1:T(8,128)S(1)} %copy.13), kind=kLoop, calls=%fused_computation.17 | loop fusion | flops 1048576 | bytes 1573632 | tf_op jit(solution)/shard_map/add | solution.py:58
  20.7 0.1 fusion.22
  20.8 0.6 %gather_fusion = bf16[16,4,128]{2,1,0:T(4,128)(2,1)S(1)} fusion(bf16[4,16,128]{2,0,1:T(4,128)(2,1)S(1)} %copy.16, s32[1024]{0:T(1024)S(1)} %pad_clamp_fusion), kind=kCustom, calls=%fused_computation | custom fusion | bytes 32832 | tf_op jit(solution)/shard_map/gather | solution.py:62
  21.4 0.0 copy-done
  21.4 0.2 fusion.9
  21.6 0.3 fusion
  22.0 1.6 %collective-permute-start.4 = (f32[4,2048]{1,0:T(4,128)S(1)}, f32[4,2048]{1,0:T(4,128)S(1)}, u32[]{:S(2)}, u32[]{:S(2)}) collective-permute-start(f32[4,2048]{1,0:T(4,128)S(1)} %bitcast.117), channel_id=1, source_target_pairs={{0,5},{1,6},{2,7},{3,0},{4,1},{5,2},{6,3},{7,4},{8,13},{9,14},{10,... | collective-permute-start | bytes 98312 | tf_op jit(solution)/shard_map/ppermute | solution.py:29
  23.7 1.4 %collective-permute-start.5 = (f32[4,2048]{1,0:T(4,128)S(1)}, f32[4,2048]{1,0:T(4,128)S(1)}, u32[]{:S(2)}, u32[]{:S(2)}) collective-permute-start(f32[4,2048]{1,0:T(4,128)S(1)} %bitcast.116), channel_id=1, source_target_pairs={{0,6},{1,7},{2,0},{3,1},{4,2},{5,3},{6,4},{7,5},{8,14},{9,15},{10,... | collective-permute-start | bytes 98312 | tf_op jit(solution)/shard_map/ppermute | solution.py:29
  25.1 1.9 %collective-permute-start.6 = (f32[4,2048]{1,0:T(4,128)S(1)}, f32[4,2048]{1,0:T(4,128)S(1)}, u32[]{:S(2)}, u32[]{:S(2)}) collective-permute-start(f32[4,2048]{1,0:T(4,128)S(1)} %bitcast.118), channel_id=1, source_target_pairs={{0,7},{1,0},{2,1},{3,2},{4,3},{5,4},{6,5},{7,6},{8,15},{9,8},{10,9... | collective-permute-start | bytes 98312 | tf_op jit(solution)/shard_map/ppermute | solution.py:29
  27.0 0.6 %collective-permute-start.7 = (f32[4,2048]{1,0:T(4,128)S(1)}, f32[4,2048]{1,0:T(4,128)S(1)}, u32[]{:S(2)}, u32[]{:S(2)}) collective-permute-start(f32[4,2048]{1,0:T(4,128)S(1)} %bitcast.119), channel_id=1, source_target_pairs={{0,1},{1,2},{2,3},{3,4},{4,5},{5,6},{6,7},{7,0},{8,9},{9,10},{10,1... | collective-permute-start | bytes 98312 | tf_op jit(solution)/shard_map/ppermute | solution.py:29
  27.6 2.1 %collective-permute-start.8 = (f32[4,2048]{1,0:T(4,128)S(1)}, f32[4,2048]{1,0:T(4,128)S(1)}, u32[]{:S(2)}, u32[]{:S(2)}) collective-permute-start(f32[4,2048]{1,0:T(4,128)S(1)} %bitcast.120), channel_id=1, source_target_pairs={{0,2},{1,3},{2,4},{3,5},{4,6},{5,7},{6,0},{7,1},{8,10},{9,11},{10,... | collective-permute-start | bytes 98312 | tf_op jit(solution)/shard_map/ppermute | solution.py:29
  29.7 0.0 collective-permute-done.4
  29.7 1.5 %collective-permute-start.9 = (f32[4,2048]{1,0:T(4,128)S(1)}, f32[4,2048]{1,0:T(4,128)S(1)}, u32[]{:S(2)}, u32[]{:S(2)}) collective-permute-start(f32[4,2048]{1,0:T(4,128)S(1)} %bitcast.121), channel_id=1, source_target_pairs={{0,3},{1,4},{2,5},{3,6},{4,7},{5,0},{6,1},{7,2},{8,11},{9,12},{10,... | collective-permute-start | bytes 98312 | tf_op jit(solution)/shard_map/ppermute | solution.py:29
  31.2 0.0 collective-permute-done.5
  31.2 0.0 collective-permute-done.6
  31.2 2.4 %collective-permute-done.7 = f32[4,2048]{1,0:T(4,128)S(1)} collective-permute-done((f32[4,2048]{1,0:T(4,128)S(1)}, f32[4,2048]{1,0:T(4,128)S(1)}, u32[]{:S(2)}, u32[]{:S(2)}) %collective-permute-start.7) | collective-permute-done | bytes 32800 | tf_op jit(solution)/shard_map/ppermute | solution.py:29
  33.6 0.0 collective-permute-done.8
  33.6 1.8 %collective-permute-done.9 = f32[4,2048]{1,0:T(4,128)S(1)} collective-permute-done((f32[4,2048]{1,0:T(4,128)S(1)}, f32[4,2048]{1,0:T(4,128)S(1)}, u32[]{:S(2)}, u32[]{:S(2)}) %collective-permute-start.9) | collective-permute-done | bytes 32800 | tf_op jit(solution)/shard_map/ppermute | solution.py:29
  35.5 0.0 copy-start.1
  35.5 0.1 collective-permute-start.10
  35.6 1.2 %collective-permute-done.10 = f32[4,2048]{1,0:T(4,128)S(1)} collective-permute-done((f32[4,2048]{1,0:T(4,128)S(1)}, f32[4,2048]{1,0:T(4,128)S(1)}, u32[]{:S(2)}, u32[]{:S(2)}) %collective-permute-start.10) | collective-permute-done | bytes 32800 | tf_op jit(solution)/shard_map/ppermute | solution.py:84
  36.8 1.7 %collective-permute-start.11 = (f32[4,2048]{1,0:T(4,128)S(1)}, f32[4,2048]{1,0:T(4,128)S(1)}, u32[]{:S(2)}, u32[]{:S(2)}) collective-permute-start(f32[4,2048]{1,0:T(4,128)S(1)} %add.89), channel_id=1, source_target_pairs={{0,16},{8,24},{16,0},{24,8},{1,17},{9,25},{17,1},{25,9},{2,18},{10... | collective-permute-start | bytes 98312 | tf_op jit(solution)/shard_map/ppermute | solution.py:84
  38.6 2.2 %collective-permute-done.11 = f32[4,2048]{1,0:T(4,128)S(1)} collective-permute-done((f32[4,2048]{1,0:T(4,128)S(1)}, f32[4,2048]{1,0:T(4,128)S(1)}, u32[]{:S(2)}, u32[]{:S(2)}) %collective-permute-start.11) | collective-permute-done | bytes 32800 | tf_op jit(solution)/shard_map/ppermute | solution.py:84
  40.8 0.1 add_dynamic-update-slice_fusion
  40.9 0.1 select_bitcast_fusion
  41.0 1.1 %copy.18 = f32[1,1,4,16,2048]{4,3,2,1,0:T(8,128)} copy(f32[1,1,4,16,2048]{4,2,3,1,0:T(4,128)S(1)} %select_bitcast_fusion) | data formatting | bytes 1048576 | tf_op jit(solution)/shard_map/broadcast_in_dim | solution.py:91
  (27 shorter events, 0.3 us)
Async XLA Ops:
  0.0 21.4 %copy-start = (bf16[1,1,16,128,128]{4,3,2,1,0:T(8,128)(2,1)S(1)}, bf16[1,1,16,128,128]{4,3,2,1,0:T(8,128)(2,1)}, u32[]{:S(2)}) copy-start(bf16[1,1,16,128,128]{4,3,2,1,0:T(8,128)(2,1)} %param.20) | copy-start | bytes 1572868
  1.5 9.5 %collective-permute-start = (f32[4,16,1]{2,0,1:T(4,128)S(1)}, f32[4,16,1]{2,0,1:T(4,128)S(1)}, u32[]{:S(2)}, u32[]{:S(2)}) collective-permute-start(f32[4,16,1]{2,0,1:T(4,128)S(1)} %get-tuple-element.35), channel_id=1, source_target_pairs={{0,1},{1,2},{2,3},{3,4},{4,5},{5,6},{6,7},{7,0},{8,9},{9,10},{10,1... | collective-permute-start | bytes 776 | tf_op jit(solution)/shard_map/ppermute | solution.py:17
  4.5 6.5 %collective-permute-start.1 = (f32[4,16,1]{2,0,1:T(4,128)S(1)}, f32[4,16,1]{2,0,1:T(4,128)S(1)}, u32[]{:S(2)}, u32[]{:S(2)}) collective-permute-start(f32[4,16,1]{2,0,1:T(4,128)S(1)} %get-tuple-element.36), channel_id=1, source_target_pairs={{1,0},{2,1},{3,2},{4,3},{5,4},{6,5},{7,6},{0,7},{9,8},{10,9},{11,1... | collective-permute-start | bytes 776 | tf_op jit(solution)/shard_map/ppermute | solution.py:19
  7.6 0.7 %copy-start.4 = (f32[2,4]{1,0:T(2,128)S(1)}, f32[2,4]{1,0:T(2,128)}, u32[]{:S(2)}) copy-start(f32[2,4]{1,0:T(2,128)} %param.16) | copy-start | bytes 100
  8.3 0.7 %copy-start.7 = (s32[1,1,16]{2,1,0:T(1,128)S(1)}, s32[1,1,16]{2,1,0:T(1,128)}, u32[]{:S(2)}) copy-start(s32[1,1,16]{2,1,0:T(1,128)} %param.17) | copy-start | bytes 196
  9.0 0.7 %copy-start.5 = (s32[1,1,16]{2,1,0:T(1,128)S(1)}, s32[1,1,16]{2,1,0:T(1,128)}, u32[]{:S(2)}) copy-start(s32[1,1,16]{2,1,0:T(1,128)} %param.18) | copy-start | bytes 196
  9.6 0.7 %copy-start.6 = (s32[1,1,16]{2,1,0:T(1,128)S(1)}, s32[1,1,16]{2,1,0:T(1,128)}, u32[]{:S(2)}) copy-start(s32[1,1,16]{2,1,0:T(1,128)} %param.19) | copy-start | bytes 196
  10.3 0.7 %copy-start.3 = (f32[2,4,16]{2,1,0:T(4,128)S(1)}, f32[2,4,16]{2,1,0:T(4,128)}, u32[]{:S(2)}) copy-start(f32[2,4,16]{2,1,0:T(4,128)} %param.14) | copy-start | bytes 1540
  11.8 6.6 %collective-permute-start.2 = (f32[4,16,1]{2,0,1:T(4,128)S(1)}, f32[4,16,1]{2,0,1:T(4,128)S(1)}, u32[]{:S(2)}, u32[]{:S(2)}) collective-permute-start(f32[4,16,1]{2,0,1:T(4,128)S(1)} %get-tuple-element.33), channel_id=1, source_target_pairs={{0,1},{1,2},{2,3},{3,4},{4,5},{5,6},{6,7},{7,0},{8,9},{9,10},{10,1... | collective-permute-start | bytes 776 | tf_op jit(solution)/shard_map/ppermute | solution.py:17
  11.8 6.6 %collective-permute-start.3 = (f32[4,16,1]{2,0,1:T(4,128)S(1)}, f32[4,16,1]{2,0,1:T(4,128)S(1)}, u32[]{:S(2)}, u32[]{:S(2)}) collective-permute-start(f32[4,16,1]{2,0,1:T(4,128)S(1)} %get-tuple-element.34), channel_id=1, source_target_pairs={{1,0},{2,1},{3,2},{4,3},{5,4},{6,5},{7,6},{0,7},{9,8},{10,9},{11,1... | collective-permute-start | bytes 776 | tf_op jit(solution)/shard_map/ppermute | solution.py:19
  16.5 2.5 %copy-start.2 = (f32[2,16,16]{2,1,0:T(8,128)S(1)}, f32[2,16,16]{2,1,0:T(8,128)}, u32[]{:S(2)}) copy-start(f32[2,16,16]{2,1,0:T(8,128)} %param.15) | copy-start | bytes 6148
  22.0 7.7 %collective-permute-start.4 = (f32[4,2048]{1,0:T(4,128)S(1)}, f32[4,2048]{1,0:T(4,128)S(1)}, u32[]{:S(2)}, u32[]{:S(2)}) collective-permute-start(f32[4,2048]{1,0:T(4,128)S(1)} %bitcast.117), channel_id=1, source_target_pairs={{0,5},{1,6},{2,7},{3,0},{4,1},{5,2},{6,3},{7,4},{8,13},{9,14},{10,... | collective-permute-start | bytes 98312 | tf_op jit(solution)/shard_map/ppermute | solution.py:29
  23.7 7.5 %collective-permute-start.5 = (f32[4,2048]{1,0:T(4,128)S(1)}, f32[4,2048]{1,0:T(4,128)S(1)}, u32[]{:S(2)}, u32[]{:S(2)}) collective-permute-start(f32[4,2048]{1,0:T(4,128)S(1)} %bitcast.116), channel_id=1, source_target_pairs={{0,6},{1,7},{2,0},{3,1},{4,2},{5,3},{6,4},{7,5},{8,14},{9,15},{10,... | collective-permute-start | bytes 98312 | tf_op jit(solution)/shard_map/ppermute | solution.py:29
  25.1 6.1 %collective-permute-start.6 = (f32[4,2048]{1,0:T(4,128)S(1)}, f32[4,2048]{1,0:T(4,128)S(1)}, u32[]{:S(2)}, u32[]{:S(2)}) collective-permute-start(f32[4,2048]{1,0:T(4,128)S(1)} %bitcast.118), channel_id=1, source_target_pairs={{0,7},{1,0},{2,1},{3,2},{4,3},{5,4},{6,5},{7,6},{8,15},{9,8},{10,9... | collective-permute-start | bytes 98312 | tf_op jit(solution)/shard_map/ppermute | solution.py:29
  27.0 6.7 %collective-permute-start.7 = (f32[4,2048]{1,0:T(4,128)S(1)}, f32[4,2048]{1,0:T(4,128)S(1)}, u32[]{:S(2)}, u32[]{:S(2)}) collective-permute-start(f32[4,2048]{1,0:T(4,128)S(1)} %bitcast.119), channel_id=1, source_target_pairs={{0,1},{1,2},{2,3},{3,4},{4,5},{5,6},{6,7},{7,0},{8,9},{9,10},{10,1... | collective-permute-start | bytes 98312 | tf_op jit(solution)/shard_map/ppermute | solution.py:29
  27.6 6.0 %collective-permute-start.8 = (f32[4,2048]{1,0:T(4,128)S(1)}, f32[4,2048]{1,0:T(4,128)S(1)}, u32[]{:S(2)}, u32[]{:S(2)}) collective-permute-start(f32[4,2048]{1,0:T(4,128)S(1)} %bitcast.120), channel_id=1, source_target_pairs={{0,2},{1,3},{2,4},{3,5},{4,6},{5,7},{6,0},{7,1},{8,10},{9,11},{10,... | collective-permute-start | bytes 98312 | tf_op jit(solution)/shard_map/ppermute | solution.py:29
  29.7 5.8 %collective-permute-start.9 = (f32[4,2048]{1,0:T(4,128)S(1)}, f32[4,2048]{1,0:T(4,128)S(1)}, u32[]{:S(2)}, u32[]{:S(2)}) collective-permute-start(f32[4,2048]{1,0:T(4,128)S(1)} %bitcast.121), channel_id=1, source_target_pairs={{0,3},{1,4},{2,5},{3,6},{4,7},{5,0},{6,1},{7,2},{8,11},{9,12},{10,... | collective-permute-start | bytes 98312 | tf_op jit(solution)/shard_map/ppermute | solution.py:29
  35.5 3.0 %copy-start.1 = (s32[1,2048]{1,0:T(1,128)S(1)}, s32[1,2048]{1,0:T(1,128)}, u32[]{:S(2)}) copy-start(s32[1,2048]{1,0:T(1,128)} %param.21) | copy-start | bytes 24580
  35.5 1.3 %collective-permute-start.10 = (f32[4,2048]{1,0:T(4,128)S(1)}, f32[4,2048]{1,0:T(4,128)S(1)}, u32[]{:S(2)}, u32[]{:S(2)}) collective-permute-start(f32[4,2048]{1,0:T(4,128)S(1)} %fusion.19), channel_id=1, source_target_pairs={{0,8},{8,0},{16,24},{24,16},{1,9},{9,1},{17,25},{25,17},{2,10},{10... | collective-permute-start | bytes 98312 | tf_op jit(solution)/shard_map/ppermute | solution.py:84
  36.8 4.0 %collective-permute-start.11 = (f32[4,2048]{1,0:T(4,128)S(1)}, f32[4,2048]{1,0:T(4,128)S(1)}, u32[]{:S(2)}, u32[]{:S(2)}) collective-permute-start(f32[4,2048]{1,0:T(4,128)S(1)} %add.89), channel_id=1, source_target_pairs={{0,16},{8,24},{16,0},{24,8},{1,17},{9,25},{17,1},{25,9},{2,18},{10... | collective-permute-start | bytes 98312 | tf_op jit(solution)/shard_map/ppermute | solution.py:84
